TPU v7x, 32 devices: a whole 2x2x4 slice. The times are simulated.
32 devices in a mesh: gz: 8 (over z, x), gy: 4 (over y, core).
Axes of the slice: x: 2, y: 2, z: 4, core: 2. Of those that a mesh axis runs over, the one named last changes fastest.
Arguments:
- iterate: float32 [16, 256, 1024], P('gz', 'gy'), may hold values from -1.5 to 1.5
- basis: bfloat16 [32, 16, 256, 1024], P(None, 'gz', 'gy'), may hold values from -6 to 6
- coeffs: float32 [32], replicated, may hold values from -0.3125 to 0.3125
- rhs: float32 [16, 256, 1024], P('gz', 'gy'), may hold values from -8 to 8
- kappa: float32 [16, 256, 1024], P('gz', 'gy'), may hold values from 0.5 to 4
- offsets: int32 [16, 256, 8], P('gz', 'gy'), may hold values from 0 to 2047
- flips: int32 [16, 256, 8], P('gz', 'gy'), may hold values from 0 to 1
Outputs:
- new_iterate: float32 [16, 256, 1024], P('gz', 'gy')
- residual: float32 [16, 256, 1024], P('gz', 'gy')
- sketch_unit: float32 [2048], replicated
All inputs are finite; a program needn't handle non-finite values.
Results may differ from a plain program's by a relative error of at most 0.00058.
Values sent between devices are 32-bit elements; how exact they have to be, the bound alone decides.
A program may use at most 64 MiB of HBM per device.

v0:
```python
import jax
import jax.numpy as jnp
from jax import lax
from jax.sharding import PartitionSpec as P

SK = 2048
BLK = 128


def padded_2(cells, sides, width):
    for axis, dim in sides:
        count = lax.axis_size(axis)
        ends = count - 1
        head = lax.slice_in_dim(cells, 0, width, axis=dim)
        tail = lax.slice_in_dim(cells, cells.shape[dim] - width, cells.shape[dim], axis=dim)
        cells = jnp.concatenate(
            [
                lax.ppermute(tail, axis, [(i, (i + 1) % count) for i in range(ends)]),
                cells,
                lax.ppermute(head, axis, [((i + 1) % count, i) for i in range(ends)]),
            ],
            axis=dim,
        )
    return cells


def apply_operator(upad, kpad):
    field = upad[1:-1, 1:-1, :]
    coef = kpad[1:-1, 1:-1, :]
    total = 0.05 * field
    neighbours = [
        (upad[2:, 1:-1, :], kpad[2:, 1:-1, :]),
        (upad[:-2, 1:-1, :], kpad[:-2, 1:-1, :]),
        (upad[1:-1, 2:, :], kpad[1:-1, 2:, :]),
        (upad[1:-1, :-2, :], kpad[1:-1, :-2, :]),
    ]
    zero_col = jnp.zeros_like(field[:, :, :1])
    neighbours.append(
        (
            jnp.concatenate([field[:, :, 1:], zero_col], 2),
            jnp.concatenate([coef[:, :, 1:], zero_col], 2),
        )
    )
    neighbours.append(
        (
            jnp.concatenate([zero_col, field[:, :, :-1]], 2),
            jnp.concatenate([zero_col, coef[:, :, :-1]], 2),
        )
    )
    for other, kother in neighbours:
        total = total + 0.5 * (coef + kother) * (field - other)
    return total


def local_sketch(residual, offsets, flips):
    blocks = residual.reshape(-1, BLK)
    signs = (2 * flips - 1).astype(jnp.float32).reshape(-1, 1)
    columns = lax.broadcasted_iota(jnp.int32, (1, SK), 1)
    placed = jnp.where(offsets.reshape(-1, 1) == columns, signs, 0.0)
    spread = jnp.dot(
        blocks.T, placed, precision=lax.Precision.HIGHEST, preferred_element_type=jnp.float32
    )
    doubled = jnp.concatenate([spread, spread], 1).reshape(-1)
    doubled = jnp.concatenate([doubled, jnp.zeros((SK,), jnp.float32)])
    skewed = doubled[SK : SK + BLK * (2 * SK - 1)].reshape(BLK, 2 * SK - 1)
    return jnp.sum(skewed[:, :SK], axis=0)


def shards(iterate, basis, coeffs, rhs, kappa, offsets, flips):
    coeff_b = coeffs.astype(jnp.bfloat16)
    new_iterate = iterate + jnp.einsum(
        "k,kzyx->zyx", coeff_b, basis, preferred_element_type=jnp.float32
    )
    stacked = jnp.stack([new_iterate, kappa])
    padded = padded_2(stacked, (("gz", 1), ("gy", 2)), 1)
    upad = padded[0]
    kpad = padded[1]
    residual = rhs - apply_operator(upad, kpad)
    partial_sketch = local_sketch(residual, offsets, flips)
    sketch = lax.psum(partial_sketch, ("gz", "gy"))
    sketch_unit = sketch / jnp.sqrt(jnp.mean(sketch * sketch) + 1e-06)
    return (new_iterate, residual, sketch_unit)


def solution(mesh):
    return jax.shard_map(
        shards,
        mesh=mesh,
        in_specs=(
            P("gz", "gy", None),
            P(None, "gz", "gy", None),
            P(),
            P("gz", "gy", None),
            P("gz", "gy", None),
            P("gz", "gy", None),
            P("gz", "gy", None),
        ),
        out_specs=(P("gz", "gy", None), P("gz", "gy", None), P()),
        check_vma=False,
    )
```

profile of v0, /device:TPU:0, one launch (start us, length us, event | category | flops | bytes accessed | tf_op | source)
XLA Modules:
  0.0 103.9 jit_solution(8005359275835103179)
XLA Ops:
  0.7 12.6 %fusion = f32[1,2,64,1024]{3,0,2,1:T(1,128)S(1)} fusion(bf16[32,2,64,1024]{3,2,1,0:T(8,128)(2,1)} %param.8, f32[32]{0:T(128)} %param.9), kind=kOutput, calls=%fused_computation | convolution fusion | flops 8388640 | bytes 8913024 | tf_op jit(solution)/shard_map/k,kzyx->zyx/dot_general | solution.py:71
  13.2 0.1 bitcast_add_fusion
  13.5 4.9 %collective-permute-start = (f32[2,1,64,1024]{3,2,1,0:T(8,128)S(1)}, f32[2,1,64,1024]{3,2,1,0:T(8,128)S(1)}, u32[]{:S(2)}, u32[]{:S(2)}) collective-permute-start(f32[2,1,64,1024]{3,2,1,0:T(8,128)S(1)} %get-tuple-element.11), channel_id=1, source_target_pairs={{0,4},{4,8},{8,12},{12,16},{16,20},{20,24},{24,28},{1,5},{5,9},{9,... | collective-permute-start | bytes 1572872 | tf_op jit(solution)/shard_map/ppermute | solution.py:18
  18.4 1.3 %collective-permute-start.1 = (f32[2,1,64,1024]{3,2,1,0:T(8,128)S(1)}, f32[2,1,64,1024]{3,2,1,0:T(8,128)S(1)}, u32[]{:S(2)}, u32[]{:S(2)}) collective-permute-start(f32[2,1,64,1024]{3,2,1,0:T(8,128)S(1)} %get-tuple-element.12), channel_id=1, source_target_pairs={{4,0},{8,4},{12,8},{16,12},{20,16},{24,20},{28,24},{5,1},{9,5},{13... | collective-permute-start | bytes 1572872 | tf_op jit(solution)/shard_map/ppermute | solution.py:20
  19.7 21.1 %collective-permute-done = f32[2,1,64,1024]{3,2,1,0:T(8,128)S(1)} collective-permute-done((f32[2,1,64,1024]{3,2,1,0:T(8,128)S(1)}, f32[2,1,64,1024]{3,2,1,0:T(8,128)S(1)}, u32[]{:S(2)}, u32[]{:S(2)}) %collective-permute-start) | collective-permute-done | bytes 524320 | tf_op jit(solution)/shard_map/ppermute | solution.py:18
  40.8 1.3 %collective-permute-start.2 = (f32[2,4,1,1024]{3,2,1,0:T(1,128)S(1)}, f32[2,4,1,1024]{3,2,1,0:T(1,128)S(1)}, u32[]{:S(2)}, u32[]{:S(2)}) collective-permute-start(f32[2,4,1,1024]{3,2,1,0:T(1,128)S(1)} %get-tuple-element.5), channel_id=1, source_target_pairs={{0,1},{1,2},{2,3},{4,5},{5,6},{6,7},{8,9},{9,10},{10,11},{12,13},{... | collective-permute-start | bytes 98312 | tf_op jit(solution)/shard_map/ppermute | solution.py:18
  42.1 1.5 %collective-permute-start.3 = (f32[2,4,1,1024]{3,2,1,0:T(1,128)S(1)}, f32[2,4,1,1024]{3,2,1,0:T(1,128)S(1)}, u32[]{:S(2)}, u32[]{:S(2)}) collective-permute-start(f32[2,4,1,1024]{3,2,1,0:T(1,128)S(1)} %get-tuple-element.6), channel_id=1, source_target_pairs={{1,0},{2,1},{3,2},{5,4},{6,5},{7,6},{9,8},{10,9},{11,10},{13,12},{... | collective-permute-start | bytes 98312 | tf_op jit(solution)/shard_map/ppermute | solution.py:20
  43.7 0.1 broadcast_in_dim.16
  43.9 0.1 eq.15
  44.0 2.9 %collective-permute-done.3 = f32[2,4,1,1024]{3,2,1,0:T(1,128)S(1)} collective-permute-done((f32[2,4,1,1024]{3,2,1,0:T(1,128)S(1)}, f32[2,4,1,1024]{3,2,1,0:T(1,128)S(1)}, u32[]{:S(2)}, u32[]{:S(2)}) %collective-permute-start.3) | collective-permute-done | bytes 32800 | tf_op jit(solution)/shard_map/ppermute | solution.py:20
  47.0 0.3 pad_maximum_fusion
  47.3 0.2 slice_bitcast_fusion
  47.5 0.5 fusion.26
  48.0 0.6 copy-done.4
  48.5 0.8 fusion.12
  49.4 5.4 %fusion.2 = f32[128,2048]{1,0:T(8,128)S(1)} fusion(f32[1024,128]{1,0:T(8,128)S(1)} %reshape.19, f32[1024]{0:T(1024)S(1)} %broadcast_in_dim.16, s32[1024]{0:T(1024)S(1)} %eq.15), kind=kOutput, calls=%fused_computation.2 | convolution fusion | flops 3225419776 | bytes 1581056 | tf_op jit(solution)/shard_map/dot_general | solution.py:60
  54.9 0.2 maximum_bitcast_fusion
  55.1 0.4 copy.17
  55.5 0.1 pad_slice_fusion
  55.6 2.5 %reshape.21 = f32[128,4095]{1,0:T(8,128)} reshape(f32[524160]{0:T(1024)S(1)} %pad_slice_fusion) | data formatting | bytes 4193280 | tf_op jit(solution)/shard_map/reshape | solution.py:65
  58.1 1.3 %slice_reduce_fusion = f32[2048]{0:T(1024)S(1)} fusion(f32[128,4095]{1,0:T(8,128)} %reshape.21), kind=kLoop, calls=%fused_computation.13 | loop fusion | flops 260096 | bytes 1056768 | tf_op jit(solution)/shard_map/reduce_sum | solution.py:66
  59.4 42.6 %psum.7 = f32[2048]{0:T(1024)S(1)} all-reduce(f32[2048]{0:T(1024)S(1)} %slice_reduce_fusion), channel_id=1, replica_groups=mesh['gz'=8,'gy'=4] {'gz','gy'}, use_global_device_ids=true, to_apply=%region_1.2 | all-reduce | flops 2048 | bytes 16384 | tf_op jit(solution)/shard_map/psum | solution.py:80
  102.0 0.6 multiply_reduce_fusion
  103.3 0.6 broadcast_divide_fusion
  (21 shorter events, 0.4 us)
Async XLA Ops:
  0.6 12.6 %copy-start.3 = (f32[2,64,1024]{2,1,0:T(8,128)S(1)}, f32[2,64,1024]{2,1,0:T(8,128)}, u32[]{:S(2)}) copy-start(f32[2,64,1024]{2,1,0:T(8,128)} %param.7) | copy-start | bytes 1572868
  0.6 12.7 %copy-start.1 = (f32[2,64,1024]{2,1,0:T(8,128)S(1)}, f32[2,64,1024]{2,1,0:T(8,128)}, u32[]{:S(2)}) copy-start(f32[2,64,1024]{2,1,0:T(8,128)} %param.11) | copy-start | bytes 1572868
  13.3 33.9 %copy-start = (f32[2,64,1024]{2,1,0:T(8,128)}, f32[2,64,1024]{2,1,0:T(8,128)S(1)}, u32[]{:S(2)}) copy-start(f32[2,64,1024]{2,1,0:T(8,128)S(1)} %bitcast_add_fusion) | copy-start | bytes 1572868
  13.4 30.2 %copy-start.6 = (s32[2,64,8]{1,2,0:T(8,128)S(1)}, s32[2,64,8]{1,2,0:T(8,128)}, u32[]{:S(2)}) copy-start(s32[2,64,8]{1,2,0:T(8,128)} %param.13) | copy-start | bytes 12292
  13.4 30.4 %copy-start.5 = (s32[2,64,8]{1,2,0:T(8,128)S(1)}, s32[2,64,8]{1,2,0:T(8,128)}, u32[]{:S(2)}) copy-start(s32[2,64,8]{1,2,0:T(8,128)} %param.12) | copy-start | bytes 12292
  13.5 27.3 %collective-permute-start = (f32[2,1,64,1024]{3,2,1,0:T(8,128)S(1)}, f32[2,1,64,1024]{3,2,1,0:T(8,128)S(1)}, u32[]{:S(2)}, u32[]{:S(2)}) collective-permute-start(f32[2,1,64,1024]{3,2,1,0:T(8,128)S(1)} %get-tuple-element.11), channel_id=1, source_target_pairs={{0,4},{4,8},{8,12},{12,16},{16,20},{20,24},{24,28},{1,5},{5,9},{9,... | collective-permute-start | bytes 1572872 | tf_op jit(solution)/shard_map/ppermute | solution.py:18
  18.4 22.4 %collective-permute-start.1 = (f32[2,1,64,1024]{3,2,1,0:T(8,128)S(1)}, f32[2,1,64,1024]{3,2,1,0:T(8,128)S(1)}, u32[]{:S(2)}, u32[]{:S(2)}) collective-permute-start(f32[2,1,64,1024]{3,2,1,0:T(8,128)S(1)} %get-tuple-element.12), channel_id=1, source_target_pairs={{4,0},{8,4},{12,8},{16,12},{20,16},{24,20},{28,24},{5,1},{9,5},{13... | collective-permute-start | bytes 1572872 | tf_op jit(solution)/shard_map/ppermute | solution.py:20
  40.8 3.2 %collective-permute-start.2 = (f32[2,4,1,1024]{3,2,1,0:T(1,128)S(1)}, f32[2,4,1,1024]{3,2,1,0:T(1,128)S(1)}, u32[]{:S(2)}, u32[]{:S(2)}) collective-permute-start(f32[2,4,1,1024]{3,2,1,0:T(1,128)S(1)} %get-tuple-element.5), channel_id=1, source_target_pairs={{0,1},{1,2},{2,3},{4,5},{5,6},{6,7},{8,9},{9,10},{10,11},{12,13},{... | collective-permute-start | bytes 98312 | tf_op jit(solution)/shard_map/ppermute | solution.py:18
  42.1 4.9 %collective-permute-start.3 = (f32[2,4,1,1024]{3,2,1,0:T(1,128)S(1)}, f32[2,4,1,1024]{3,2,1,0:T(1,128)S(1)}, u32[]{:S(2)}, u32[]{:S(2)}) collective-permute-start(f32[2,4,1,1024]{3,2,1,0:T(1,128)S(1)} %get-tuple-element.6), channel_id=1, source_target_pairs={{1,0},{2,1},{3,2},{5,4},{6,5},{7,6},{9,8},{10,9},{11,10},{13,12},{... | collective-permute-start | bytes 98312 | tf_op jit(solution)/shard_map/ppermute | solution.py:20
  47.5 1.0 %copy-start.4 = (f32[2,64,1024]{2,1,0:T(8,128)S(1)}, f32[2,64,1024]{2,1,0:T(8,128)}, u32[]{:S(2)}) copy-start(f32[2,64,1024]{2,1,0:T(8,128)} %param.10) | copy-start | bytes 1572868
  49.3 5.6 %copy-start.2 = (f32[2,64,1024]{2,1,0:T(8,128)}, f32[2,64,1024]{2,1,0:T(8,128)S(1)}, u32[]{:S(2)}) copy-start(f32[2,64,1024]{2,1,0:T(8,128)S(1)} %fusion.12) | copy-start | bytes 1572868
where the time goes:
time: 104 us
  blocking collectives  42.6 us (41%)
  waiting for transfers between devices  24 us (23%)
  matrix products  18 us (17%)
  starting transfers between devices  8.96 us (9%)
  local copies, waits for them, and re-layouts  4.64 us (4%)
  other arithmetic  4.09 us (4%)
  between operations  1.57 us (2%)
    psum x1, blocking collectives, shards(): sketch = lax.psum(partial_sketch, ('gz', 'gy'))  42.6 us
    ppermute x2, waiting for transfers between devices, padded_2(): lax.ppermute(tail, axis, [(i, (i + 1) % count) for i in range(ends)])  21.1 us
    dot_general x1, matrix products, shards(): jnp.einsum('k,kzyx->zyx', coeff_b, basis, preferred_element_type=jnp.floa...  12.6 us
    ppermute x2, starting transfers between devices, padded_2(): lax.ppermute(tail, axis, [(i, (i + 1) % count) for i in range(ends)])  6.2 us
    dot_general x1, matrix products, local_sketch(): jnp.dot(blocks.T, placed, precision=lax.Precision.HIGHEST, preferred_elem...  5.44 us
    ppermute x2, waiting for transfers between devices, padded_2(): lax.ppermute(head, axis, [((i + 1) % count, i) for i in range(ends)])  2.95 us
    ppermute x2, starting transfers between devices, padded_2(): lax.ppermute(head, axis, [((i + 1) % count, i) for i in range(ends)])  2.76 us
    reshape x1, local copies, waits for them, and re-layouts, local_sketch(): skewed = doubled[SK:SK + BLK * (2 * SK - 1)].reshape(BLK, 2 * SK - 1)  2.47 us
  transfers between devices with their start and end apart: 4, of which 2 were waited for; matrix products, arithmetic and copies ran while one was open for 0% of the time, Pallas kernels for 0%

commit v1 on v0

v1 whole, which is shorter than its diff:
```python
import functools

import jax
import jax.numpy as jnp
from jax import lax
from jax.experimental import pallas as pl
from jax.experimental.pallas import tpu as pltpu
from jax.sharding import PartitionSpec as P

SK = 2048
MESH = pl.DeviceIdType.MESH
F32 = jnp.float32
BF16 = jnp.bfloat16


def kernel(
    n_gz, n_gy, blk, rows,
    coef, iterate, basis, rhs, kappa, offsets, flips,
    u_out, r_out, s_out,
    bas, u, k, r, uh, kh, ysend, yrecv, slots_y, slots_z, part_y, part_z,
    bas_sem, load_sem, us, ur, ks, kr, ys, yr, s1s, s1r, s2s, s2r, out_sem, uout_sem,
):
    nk, nz, ny, nx = basis.shape
    nq = nx // blk
    step = 16
    nr = ny // step
    gz = lax.axis_index("gz")
    gy = lax.axis_index("gy")
    has_dn = gz > 0
    has_up = gz < n_gz - 1
    has_lf = gy > 0
    has_rt = gy < n_gy - 1
    planes = [nz - 1] + list(range(nz - 1))

    def bas_copy(z, c):
        rws = pl.ds(pl.multiple_of(c * step, step), step)
        return pltpu.make_async_copy(
            basis.at[:, z, rws, :], bas.at[:, z, rws, :], bas_sem.at[z, c]
        )

    u_load = pltpu.make_async_copy(iterate, u.at[:, pl.ds(8, ny), :], load_sem.at[0])
    k_load = pltpu.make_async_copy(kappa, k.at[:, pl.ds(8, ny), :], load_sem.at[1])
    r_load = pltpu.make_async_copy(rhs, r, load_sem.at[2])
    u_load.start()
    for c in range(nr):
        for z in planes:
            bas_copy(z, c).start()
    k_load.start()
    r_load.start()

    barrier = pltpu.get_barrier_semaphore()

    def hail(axis, me, count):
        def body(i, carry):
            pl.semaphore_signal(
                barrier, inc=1, device_id={axis: lax.rem(me + i, count)}, device_id_type=MESH
            )
            return carry
        lax.fori_loop(1, count, body, 0)

    hail("gz", gz, n_gz)
    hail("gy", gy, n_gy)
    pl.semaphore_wait(barrier, n_gz - 1 + n_gy - 1)

    up = {"gz": lax.rem(gz + 1, n_gz)}
    dn = {"gz": lax.rem(gz + n_gz - 1, n_gz)}
    rt = {"gy": lax.rem(gy + 1, n_gy)}
    lf = {"gy": lax.rem(gy + n_gy - 1, n_gy)}

    def remote(src, dst, ssem, rsem, dev):
        return pltpu.make_async_remote_copy(
            src_ref=src, dst_ref=dst, send_sem=ssem, recv_sem=rsem,
            device_id=dev, device_id_type=MESH,
        )

    def k_send(side):
        return remote(
            kappa.at[nz - 1 if side == 0 else 0], kh.at[side],
            ks.at[side], kr.at[side], up if side == 0 else dn,
        )

    def u_send(side, c):
        base = pl.multiple_of(c * step, step)
        return remote(
            u.at[nz - 1 if side == 0 else 0, pl.ds(8 + base, step), :],
            uh.at[side, pl.ds(base, step), :],
            us.at[side, c], ur.at[side, c], up if side == 0 else dn,
        )

    def y_send(side):
        return remote(
            ysend.at[side], yrecv.at[side], ys.at[side], yr.at[side],
            rt if side == 0 else lf,
        )

    z_out = (has_up, has_dn)
    z_in = (has_dn, has_up)
    y_out = (has_rt, has_lf)
    y_in = (has_lf, has_rt)
    for side in range(2):
        @pl.when(z_out[side])
        def _(side=side):
            k_send(side).start()

    u_load.wait()

    def combine(c, carry):
        for z in planes:
            base = pl.multiple_of(c * step, step)
            bas_copy(z, c).wait()
            acc = u[z, pl.ds(8 + base, step), :]
            for j in range(nk):
                acc = acc + coef[j] * bas[j, z, pl.ds(base, step), :].astype(F32)
            u[z, pl.ds(8 + base, step), :] = acc
            for side in range(2):
                if z == (nz - 1 if side == 0 else 0):
                    @pl.when(z_out[side])
                    def _(side=side):
                        u_send(side, c).start()
        return carry

    lax.fori_loop(0, nr, combine, 0)
    u_save = pltpu.make_async_copy(u.at[:, pl.ds(8, ny), :], u_out, uout_sem.at[0])
    u_save.start()
    k_load.wait()
    for side in range(2):
        row = 8 + (ny - 1 if side == 0 else 0)
        for z in range(nz):
            ysend[side, z : z + 1, :] = u[z, row : row + 1, :]
            ysend[side, nz + z : nz + z + 1, :] = k[z, row : row + 1, :]

        @pl.when(y_out[side])
        def _(side=side):
            y_send(side).start()

    for side in range(2):
        @pl.when(jnp.logical_not(z_in[side]))
        def _(side=side):
            uh[side] = jnp.zeros((ny, nx), F32)
            kh[side] = jnp.zeros((ny, nx), F32)

    r_load.wait()
    for side in range(2):
        row = 7 if side == 0 else 8 + ny

        @pl.when(y_in[side])
        def _(side=side, row=row):
            y_send(side).wait_recv()
            for z in range(nz):
                u[z, row : row + 1, :] = yrecv[side, z : z + 1, :]
                k[z, row : row + 1, :] = yrecv[side, nz + z : nz + z + 1, :]

        @pl.when(jnp.logical_not(y_in[side]))
        def _(row=row):
            for z in range(nz):
                u[z, row : row + 1, :] = jnp.zeros((1, nx), F32)
                k[z, row : row + 1, :] = jnp.zeros((1, nx), F32)

    lane = lax.broadcasted_iota(jnp.int32, (step, nx), 1)
    for c in range(nr):
        y0 = 8 + c * step
        for z in range(nz):
            uc = u[z, y0 : y0 + step, :]
            kc = k[z, y0 : y0 + step, :]

            def flux(ku, uu):
                return (kc + ku) * (uc - uu)

            ur_ = jnp.where(lane == nx - 1, 0.0, pltpu.roll(uc, nx - 1, 1))
            kr_ = jnp.where(lane == nx - 1, 0.0, pltpu.roll(kc, nx - 1, 1))
            fx = flux(kr_, ur_)
            tot = fx - jnp.where(lane == 0, -(kc * uc), pltpu.roll(fx, 1, 1))
            tot = tot + flux(k[z, y0 - 1 : y0 + step - 1, :], u[z, y0 - 1 : y0 + step - 1, :])
            tot = tot + flux(k[z, y0 + 1 : y0 + step + 1, :], u[z, y0 + 1 : y0 + step + 1, :])
            if z > 0:
                tot = tot + flux(k[z - 1, y0 : y0 + step, :], u[z - 1, y0 : y0 + step, :])
            if z < nz - 1:
                tot = tot + flux(k[z + 1, y0 : y0 + step, :], u[z + 1, y0 : y0 + step, :])
            sl = slice(c * step, (c + 1) * step)
            r[z, sl, :] = r[z, sl, :] - 0.05 * uc - 0.5 * tot

    for side in range(2):
        @pl.when(z_in[side])
        def _(side=side):
            k_send(side).wait_recv()

    col = lax.broadcasted_iota(jnp.int32, (step, blk), 1)

    def r_save(z, c):
        rws = pl.ds(pl.multiple_of(c * step, step), step)
        return pltpu.make_async_copy(r.at[z, rws, :], r_out.at[z, rws, :], out_sem.at[z, c])

    def finish(c, total):
        base = pl.multiple_of(c * step, step)
        rws = pl.ds(base, step)
        for side in range(2):
            @pl.when(z_in[side])
            def _(side=side):
                u_send(side, c).wait_recv()
        for z in range(nz):
            uc = u[z, pl.ds(8 + base, step), :]
            kc = k[z, pl.ds(8 + base, step), :]
            res = r[z, rws, :]
            if z == 0:
                res = res - 0.5 * ((kc + kh[0, rws, :]) * (uc - uh[0, rws, :]))
            if z == nz - 1:
                res = res - 0.5 * ((kc + kh[1, rws, :]) * (uc - uh[1, rws, :]))
            r[z, rws, :] = res
            r_save(z, c).start()
            off = offsets[pl.ds(pl.multiple_of(z * ny + base, step), step), :]
            flip = flips[pl.ds(pl.multiple_of(z * ny + base, step), step), :]
            sign = (2 * flip - 1).astype(F32)
            vals = []
            hots = []
            for q in range(nq):
                o = jnp.broadcast_to(off[:, q : q + 1], (step, blk))
                s = jnp.broadcast_to(sign[:, q : q + 1], (step, blk))
                x = res[:, q * blk : (q + 1) * blk] * s
                low = lax.rem(o, blk)
                bit = 1
                while bit < blk:
                    x = jnp.where((low & bit) != 0, pltpu.roll(x, bit, 1), x)
                    bit *= 2
                hi = o // blk
                nxt = jnp.where(hi == rows - 1, 0, hi + 1)
                keep = col >= low
                vals.append(jnp.where(keep, x, 0.0))
                vals.append(jnp.where(keep, 0.0, x))
                hots.append(jnp.where(col == hi, 1.0, 0.0).astype(BF16))
                hots.append(jnp.where(col == nxt, 1.0, 0.0).astype(BF16))
            val = jnp.concatenate(vals, 0)
            hot = jnp.concatenate(hots, 0)
            big = val.astype(BF16)
            small = (val - big.astype(F32)).astype(BF16)
            dims = (((0,), (0,)), ((), ()))
            total = total + lax.dot_general(hot, big, dims, preferred_element_type=F32)
            total = total + lax.dot_general(hot, small, dims, preferred_element_type=F32)
        return total

    total = lax.fori_loop(0, nr, finish, jnp.zeros((blk, blk), F32))

    def reduce(mine, axis, me, count, part, slots, ssem, rsem):
        part[...] = mine
        slots[me] = mine

        def send(i):
            dev = lax.rem(me + i, count)
            return remote(part, slots.at[me], ssem.at[i], rsem.at[me], {axis: dev})

        def take(i):
            src = lax.rem(me + i, count)
            return remote(part, slots.at[src], ssem.at[i], rsem.at[src], {axis: src})

        def go(i, carry):
            send(i).start()
            return carry

        def land(i, carry):
            take(i).wait_recv()
            return carry

        lax.fori_loop(1, count, go, 0)
        lax.fori_loop(1, count, land, 0)
        return lax.fori_loop(0, count, lambda i, acc: acc + slots[i], jnp.zeros_like(mine))

    total = reduce(total[:rows], "gy", gy, n_gy, part_y, slots_y, s1s, s1r)
    total = reduce(total, "gz", gz, n_gz, part_z, slots_z, s2s, s2r)
    mean = jnp.sum(total * total) / (rows * blk)
    s_out[...] = total / jnp.sqrt(jnp.full((rows, blk), mean, F32) + 1e-06)

    u_save.wait()
    for side in range(2):
        @pl.when(z_out[side])
        def _(side=side):
            k_send(side).wait_send()
            lax.fori_loop(0, nr, lambda c, x: (u_send(side, c).wait_send(), x)[1], 0)

        @pl.when(y_out[side])
        def _(side=side):
            y_send(side).wait_send()

    def drain(c, carry):
        for z in range(nz):
            r_save(z, c).wait()
        return carry

    lax.fori_loop(0, nr, drain, 0)

    def sent(axis, me, count, part, slots, ssem, rsem):
        def body(i, carry):
            dev = lax.rem(me + i, count)
            remote(part, slots.at[me], ssem.at[i], rsem.at[me], {axis: dev}).wait_send()
            return carry
        lax.fori_loop(1, count, body, 0)

    sent("gy", gy, n_gy, part_y, slots_y, s1s, s1r)
    sent("gz", gz, n_gz, part_z, slots_z, s2s, s2r)


def shards(n_gz, n_gy, iterate, basis, coeffs, rhs, kappa, offsets, flips):
    nk, nz, ny, nx = basis.shape
    nq = offsets.shape[-1]
    blk = nx // nq
    rows = SK // blk
    nr = ny // 16
    coef = lax.reduce_precision(coeffs, 8, 7)
    dma = pltpu.SemaphoreType.DMA
    hbm = pl.BlockSpec(memory_space=pl.ANY)
    vmem = pl.BlockSpec(memory_space=pltpu.VMEM)
    u, r, s = pl.pallas_call(
        functools.partial(kernel, n_gz, n_gy, blk, rows),
        out_shape=(
            jax.ShapeDtypeStruct((nz, ny, nx), F32),
            jax.ShapeDtypeStruct((nz, ny, nx), F32),
            jax.ShapeDtypeStruct((rows, blk), F32),
        ),
        in_specs=[pl.BlockSpec(memory_space=pltpu.SMEM), hbm, hbm, hbm, hbm, vmem, vmem],
        out_specs=(hbm, hbm, vmem),
        scratch_shapes=[
            pltpu.VMEM((nk, nz, ny, nx), BF16),
            pltpu.VMEM((nz, ny + 16, nx), F32),
            pltpu.VMEM((nz, ny + 16, nx), F32),
            pltpu.VMEM((nz, ny, nx), F32),
            pltpu.VMEM((2, ny, nx), F32),
            pltpu.VMEM((2, ny, nx), F32),
            pltpu.VMEM((2, 2 * nz, nx), F32),
            pltpu.VMEM((2, 2 * nz, nx), F32),
            pltpu.VMEM((n_gy, rows, blk), F32),
            pltpu.VMEM((n_gz, rows, blk), F32),
            pltpu.VMEM((rows, blk), F32),
            pltpu.VMEM((rows, blk), F32),
            dma((nz, nr)),
            dma((3,)),
            dma((2, nr)),
            dma((2, nr)),
            dma((2,)),
            dma((2,)),
            dma((2,)),
            dma((2,)),
            dma((n_gy,)),
            dma((n_gy,)),
            dma((n_gz,)),
            dma((n_gz,)),
            dma((nz, nr)),
            dma((1,)),
        ],
        compiler_params=pltpu.CompilerParams(collective_id=0, has_side_effects=True),
    )(
        coef, iterate, basis, rhs, kappa,
        offsets.reshape(nz * ny, nq), flips.reshape(nz * ny, nq),
    )
    return u, r, s.reshape(SK)


def solution(mesh):
    field = P("gz", "gy", None)
    return jax.shard_map(
        functools.partial(shards, mesh.shape["gz"], mesh.shape["gy"]),
        mesh=mesh,
        in_specs=(field, P(None, "gz", "gy", None), P(), field, field, field, field),
        out_specs=(field, field, P()),
        check_vma=False,
    )
```

time: 104 us -> 49.7 us (0.48)
  blocking collectives: 42.6 us -> 0 us
  Pallas kernels: 0 us -> 39.6 us
  waiting for transfers between devices: 24 us -> 0 us
  matrix products: 18 us -> 0 us
  starting transfers between devices: 8.96 us -> 0 us
  local copies, waits for them, and re-layouts: 4.64 us -> 7.91 us
  other arithmetic: 4.09 us -> 1.17 us
    psum x1 -> x0, blocking collectives: 42.6 us -> none  [shards(): sketch = lax.psum(partial_sketch, ('gz', 'gy'))]
    pallas_call x0 -> x1, Pallas kernels: none -> 39.6 us  [shards(): pl.pallas_call(functools.partial(kernel, n_gz, n_gy, blk, rows), out_shap...]
    ppermute x4 -> x0, waiting for transfers between devices: 24 us -> none  [the longest x2 21.1 us: padded_2(): lax.ppermute(tail, axis, [(i, (i + 1) % count) for i in range(ends)])]
    dot_general x2 -> x0, matrix products: 18 us -> none  [the longest x1 12.6 us: shards(): jnp.einsum('k,kzyx->zyx', coeff_b, basis, preferred_element_type=jnp.floa...]
    ppermute x4 -> x0, starting transfers between devices: 8.96 us -> none  [the longest x2 6.2 us: padded_2(): lax.ppermute(tail, axis, [(i, (i + 1) % count) for i in range(ends)])]
    unnamed x16 -> x5, local copies, waits for them, and re-layouts: 1.05 us -> 7.91 us
    reshape x2 -> x0, local copies, waits for them, and re-layouts: 2.55 us -> none  [the longest x1 2.47 us: local_sketch(): skewed = doubled[SK:SK + BLK * (2 * SK - 1)].reshape(BLK, 2 * SK - 1)]
    reduce_sum x2 -> x0, other arithmetic: 1.89 us -> none  [the longest x1 1.29 us: local_sketch(): return jnp.sum(skewed[:, :SK], axis=0)]
  transfers between devices with their start and end apart: 4 -> 0, of which waited for: 2 -> 0; matrix products, arithmetic and copies ran while one was open for 0% -> 0% of each run, Pallas kernels for 0% -> 0%
where the time goes in v1:
time: 49.7 us; the launch traced here: 49.3 us
  Pallas kernels  39.6 us (80%)
  local copies, waits for them, and re-layouts  7.91 us (16%)
  other arithmetic  1.17 us (2%)
  between operations  0.64 us (1%)
    pallas_call x1, Pallas kernels, shards(): pl.pallas_call(functools.partial(kernel, n_gz, n_gy, blk, rows), out_shap...  39.6 us
    unnamed x5, local copies, waits for them, and re-layouts  7.91 us
    reduce_precision x1, other arithmetic, shards(): coef = lax.reduce_precision(coeffs, 8, 7)  1.17 us

profile of v1, /device:TPU:0, one launch (start us, length us, event | category | flops | bytes accessed | tf_op | source)
XLA Modules:
  0.0 49.3 jit_solution(12681830053034923200)
XLA Ops:
  0.6 1.2 %reduce_precision.3.coef = f32[32]{0:T(128)} reduce-precision(f32[32]{0:T(128)} %param.9), exponent_bits=8, mantissa_bits=7 | non-fusion elementwise | flops 32 | bytes 256 | tf_op jit(solution)/shard_map/reduce_precision | solution.py:306
  1.8 1.4 %copy.10 = s32[2,64,8]{2,1,0:T(8,128)} copy(s32[2,64,8]{1,2,0:T(8,128)} %param.12) | data formatting | bytes 8192 | tf_op args[5]
  3.2 1.4 %copy.11 = s32[2,64,8]{2,1,0:T(8,128)} copy(s32[2,64,8]{1,2,0:T(8,128)} %param.13) | data formatting | bytes 8192 | tf_op args[6]
  4.6 39.6 %shard_map.94 = (f32[2,64,1024]{2,1,0:T(8,128)}, f32[2,64,1024]{2,1,0:T(8,128)}, f32[16,128]{1,0:T(8,128)}) custom-call(f32[32]{0:T(128)} %reduce_precision.3.coef, f32[2,64,1024]{2,1,0:T(8,128)} %iterate.1, bf16[32,2,64,1024]{3,2,1,0:T(8,128)(2,1)} %basis.1, f32[2,64,1024]{2,1,0:T(8,128)} %rhs.1, f32[2,64,1024]{2,1,0:T(8,128)} %kappa.1, s32[128,8]{1,0:T(8,128)} %bitcast.3, ...), custom_call_target="tpu_custom_call" | custom-call | tf_op jit(solution)/shard_map/pallas_call | solution.py:310
  44.3 1.9 %copy.15 = f32[2,64,1024]{2,1,0:T(8,128)} copy(f32[2,64,1024]{2,1,0:T(8,128)} %get-tuple-element.12) | data formatting | bytes 1048576
  46.2 1.9 %copy.16 = f32[2,64,1024]{2,1,0:T(8,128)} copy(f32[2,64,1024]{2,1,0:T(8,128)} %get-tuple-element.13) | data formatting | bytes 1048576
  48.1 1.3 %copy.17 = f32[2048]{0:T(1024)} copy(f32[2048]{0:T(1024)} %bitcast.5) | data formatting | bytes 16384

commit v2 on v1

--- a/solution.py
+++ b/solution.py
@@ -17,20 +17,29 @@
     n_gz, n_gy, blk, rows,
     coef, iterate, basis, rhs, kappa, offsets, flips,
     u_out, r_out, s_out,
-    bas, u, k, r, uh, kh, ysend, yrecv, slots_y, slots_z, part_y, part_z,
-    bas_sem, load_sem, us, ur, ks, kr, ys, yr, s1s, s1r, s2s, s2r, out_sem, uout_sem,
+    bas, cf, u, k, r, uh, kh, tf, th, oh, offc, sgnc, ysend, yrecv,
+    slots_y, slots_z, part_y, part_z,
+    bas_sem, load_sem, us, ur, ks, kr, fs, fr, os_, or_, ys, yr, s1s, s1r, s2s, s2r,
+    out_sem, uout_sem,
 ):
     nk, nz, ny, nx = basis.shape
     nq = nx // blk
+    shift = blk.bit_length() - 1
     step = 16
     nr = ny // step
+    half = nr // 2
+    hrows = half * step
+    assert nz >= 2 and ny == 2 * hrows and blk == 1 << shift
     gz = lax.axis_index("gz")
     gy = lax.axis_index("gy")
     has_dn = gz > 0
     has_up = gz < n_gz - 1
     has_lf = gy > 0
     has_rt = gy < n_gy - 1
-    planes = [nz - 1] + list(range(nz - 1))
+    top = nz - 1
+
+    def at(c):
+        return pl.multiple_of(c * step, step)
 
     def bas_copy(z, c):
         rws = pl.ds(pl.multiple_of(c * step, step), step)
@@ -42,9 +51,15 @@
     k_load = pltpu.make_async_copy(kappa, k.at[:, pl.ds(8, ny), :], load_sem.at[1])
     r_load = pltpu.make_async_copy(rhs, r, load_sem.at[2])
     u_load.start()
-    for c in range(nr):
-        for z in planes:
-            bas_copy(z, c).start()
+    for i in range(half):
+        bas_copy(top, i).start()
+        bas_copy(0, half + i).start()
+    for i in range(half):
+        bas_copy(top, half + i).start()
+        bas_copy(0, i).start()
+        for z in range(1, top):
+            bas_copy(z, i).start()
+            bas_copy(z, half + i).start()
     k_load.start()
     r_load.start()
 
@@ -73,18 +88,34 @@
             device_id=dev, device_id_type=MESH,
         )
 
+    sent_plane = (top, 0)
+    sent_row = (0, hrows)
+    toward = (up, dn)
+
     def k_send(side):
         return remote(
-            kappa.at[nz - 1 if side == 0 else 0], kh.at[side],
-            ks.at[side], kr.at[side], up if side == 0 else dn,
-        )
-
-    def u_send(side, c):
-        base = pl.multiple_of(c * step, step)
+            kappa.at[sent_plane[side], pl.ds(sent_row[side], hrows), :], kh.at[side],
+            ks.at[side], kr.at[side], toward[side],
+        )
+
+    def o_send(side, which):
+        src = (offsets, flips)[which]
         return remote(
-            u.at[nz - 1 if side == 0 else 0, pl.ds(8 + base, step), :],
-            uh.at[side, pl.ds(base, step), :],
-            us.at[side, c], ur.at[side, c], up if side == 0 else dn,
+            src.at[sent_plane[side]], oh.at[side, which],
+            os_.at[side, which], or_.at[side, which], toward[side],
+        )
+
+    def u_send(side, i):
+        return remote(
+            u.at[sent_plane[side], pl.ds(8 + sent_row[side] + at(i), step), :],
+            uh.at[side, pl.ds(at(i), step), :],
+            us.at[side, i], ur.at[side, i], toward[side],
+        )
+
+    def f_send(side, i):
+        return remote(
+            tf.at[side, pl.ds(at(i), step), :], th.at[1 - side, pl.ds(at(i), step), :],
+            fs.at[side, i], fr.at[1 - side, i], toward[1 - side],
         )
 
     def y_send(side):
@@ -101,25 +132,40 @@
         @pl.when(z_out[side])
         def _(side=side):
             k_send(side).start()
-
+            for which in range(2):
+                o_send(side, which).start()
+
+    for j in range(nk):
+        cf[j] = jnp.full((step, blk), coef[j], F32).astype(BF16).astype(F32)
     u_load.wait()
 
-    def combine(c, carry):
-        for z in planes:
-            base = pl.multiple_of(c * step, step)
-            bas_copy(z, c).wait()
-            acc = u[z, pl.ds(8 + base, step), :]
-            for j in range(nk):
-                acc = acc + coef[j] * bas[j, z, pl.ds(base, step), :].astype(F32)
-            u[z, pl.ds(8 + base, step), :] = acc
-            for side in range(2):
-                if z == (nz - 1 if side == 0 else 0):
-                    @pl.when(z_out[side])
-                    def _(side=side):
-                        u_send(side, c).start()
+    def combine(z, c):
+        bas_copy(z, c).wait()
+        acc = u[z, pl.ds(8 + at(c), step), :]
+        for j in range(nk):
+            cj = jnp.concatenate([cf[j]] * nq, 1)
+            acc = acc + cj * bas[j, z, pl.ds(at(c), step), :].astype(F32)
+        u[z, pl.ds(8 + at(c), step), :] = acc
+
+    def first(i, carry):
+        for side in range(2):
+            combine(sent_plane[side], i + side * half)
+
+            @pl.when(z_out[side])
+            def _(side=side):
+                u_send(side, i).start()
         return carry
 
-    lax.fori_loop(0, nr, combine, 0)
+    def second(i, carry):
+        combine(top, half + i)
+        combine(0, i)
+        for z in range(1, top):
+            combine(z, i)
+            combine(z, half + i)
+        return carry
+
+    lax.fori_loop(0, half, first, 0)
+    lax.fori_loop(0, half, second, 0)
     u_save = pltpu.make_async_copy(u.at[:, pl.ds(8, ny), :], u_out, uout_sem.at[0])
     u_save.start()
     k_load.wait()
@@ -136,8 +182,10 @@
     for side in range(2):
         @pl.when(jnp.logical_not(z_in[side]))
         def _(side=side):
-            uh[side] = jnp.zeros((ny, nx), F32)
-            kh[side] = jnp.zeros((ny, nx), F32)
+            uh[side] = jnp.zeros((hrows, nx), F32)
+            kh[side] = jnp.zeros((hrows, nx), F32)
+            th[side] = jnp.zeros((hrows, nx), F32)
+            oh[side] = jnp.zeros((2, nq, ny), jnp.int32)
 
     r_load.wait()
     for side in range(2):
@@ -180,66 +228,123 @@
             r[z, sl, :] = r[z, sl, :] - 0.05 * uc - 0.5 * tot
 
     for side in range(2):
+        @pl.when(jnp.logical_not(z_in[side]))
+        def _(side=side):
+            z = (0, top)[side]
+            row = hrows - sent_row[side]
+            far = slice(row, row + hrows)
+            beyond = slice(8 + row, 8 + row + hrows)
+            r[z, far, :] = r[z, far, :] - 0.5 * (k[z, beyond, :] * u[z, beyond, :])
+
+    def columns(p, off, flip):
+        offc[p] = off.T
+        sgnc[p] = (2 * flip - 1).astype(F32).T
+
+    for z in range(nz):
+        columns(z, offsets[z], flips[z])
+    for side in range(2):
         @pl.when(z_in[side])
         def _(side=side):
+            for which in range(2):
+                o_send(side, which).wait_recv()
             k_send(side).wait_recv()
+        columns(nz + side, oh[side, 0], oh[side, 1])
 
     col = lax.broadcasted_iota(jnp.int32, (step, blk), 1)
 
     def r_save(z, c):
-        rws = pl.ds(pl.multiple_of(c * step, step), step)
+        rws = pl.ds(at(c), step)
         return pltpu.make_async_copy(r.at[z, rws, :], r_out.at[z, rws, :], out_sem.at[z, c])
 
-    def finish(c, total):
-        base = pl.multiple_of(c * step, step)
-        rws = pl.ds(base, step)
-        for side in range(2):
-            @pl.when(z_in[side])
-            def _(side=side):
-                u_send(side, c).wait_recv()
-        for z in range(nz):
-            uc = u[z, pl.ds(8 + base, step), :]
-            kc = k[z, pl.ds(8 + base, step), :]
-            res = r[z, rws, :]
-            if z == 0:
-                res = res - 0.5 * ((kc + kh[0, rws, :]) * (uc - uh[0, rws, :]))
-            if z == nz - 1:
-                res = res - 0.5 * ((kc + kh[1, rws, :]) * (uc - uh[1, rws, :]))
-            r[z, rws, :] = res
-            r_save(z, c).start()
-            off = offsets[pl.ds(pl.multiple_of(z * ny + base, step), step), :]
-            flip = flips[pl.ds(pl.multiple_of(z * ny + base, step), step), :]
-            sign = (2 * flip - 1).astype(F32)
-            vals = []
-            hots = []
+    def sketch(parts):
+        vals = []
+        hots = []
+        for x_all, p, c in parts:
+            off = offc[p, pl.ds(at(c), step), :]
+            sgn = sgnc[p, pl.ds(at(c), step), :]
             for q in range(nq):
                 o = jnp.broadcast_to(off[:, q : q + 1], (step, blk))
-                s = jnp.broadcast_to(sign[:, q : q + 1], (step, blk))
-                x = res[:, q * blk : (q + 1) * blk] * s
-                low = lax.rem(o, blk)
+                s = jnp.broadcast_to(sgn[:, q : q + 1], (step, blk))
+                x = x_all[:, q * blk : (q + 1) * blk] * s
+                low = o & (blk - 1)
                 bit = 1
                 while bit < blk:
                     x = jnp.where((low & bit) != 0, pltpu.roll(x, bit, 1), x)
                     bit *= 2
-                hi = o // blk
+                hi = lax.shift_right_logical(o, shift)
                 nxt = jnp.where(hi == rows - 1, 0, hi + 1)
                 keep = col >= low
                 vals.append(jnp.where(keep, x, 0.0))
                 vals.append(jnp.where(keep, 0.0, x))
                 hots.append(jnp.where(col == hi, 1.0, 0.0).astype(BF16))
                 hots.append(jnp.where(col == nxt, 1.0, 0.0).astype(BF16))
-            val = jnp.concatenate(vals, 0)
-            hot = jnp.concatenate(hots, 0)
-            big = val.astype(BF16)
-            small = (val - big.astype(F32)).astype(BF16)
-            dims = (((0,), (0,)), ((), ()))
-            total = total + lax.dot_general(hot, big, dims, preferred_element_type=F32)
-            total = total + lax.dot_general(hot, small, dims, preferred_element_type=F32)
-        return total
-
-    total = lax.fori_loop(0, nr, finish, jnp.zeros((blk, blk), F32))
-
-    def reduce(mine, axis, me, count, part, slots, ssem, rsem):
+        val = jnp.concatenate(vals, 0)
+        hot = jnp.concatenate(hots, 0)
+        big = val.astype(BF16)
+        small = (val - big.astype(F32)).astype(BF16)
+        dims = (((0,), (0,)), ((), ()))
+        return lax.dot_general(hot, big, dims, preferred_element_type=F32) + lax.dot_general(
+            hot, small, dims, preferred_element_type=F32
+        )
+
+    def early(i, total):
+        parts = [(r[top, pl.ds(at(i), step), :], top, i)]
+        parts.append((r[0, pl.ds(at(half + i), step), :], 0, half + i))
+        for z in range(1, top):
+            for c in (i, half + i):
+                parts.append((r[z, pl.ds(at(c), step), :], z, c))
+                r_save(z, c).start()
+        return total + sketch(parts)
+
+    total = lax.fori_loop(0, half, early, jnp.zeros((blk, blk), F32))
+    real = [jnp.where(z_in[side], 1.0, 0.0) for side in range(2)]
+
+    def finish(i, total):
+        parts = []
+        for side in range(2):
+            z = (0, top)[side]
+            c = i + side * half
+
+            @pl.when(z_in[side])
+            def _(side=side):
+                u_send(side, i).wait_recv()
+
+            uc = u[z, pl.ds(8 + at(c), step), :]
+            kc = k[z, pl.ds(8 + at(c), step), :]
+            rws = pl.ds(at(i), step)
+            t = 0.5 * ((kc + kh[side, rws, :]) * (uc - uh[side, rws, :]))
+            tf[side, rws, :] = t
+
+            @pl.when(z_in[side])
+            def _(side=side):
+                f_send(side, i).start()
+
+            res = r[z, pl.ds(at(c), step), :] - t
+            r[z, pl.ds(at(c), step), :] = res
+            r_save(z, c).start()
+            parts.append((res, z, c))
+            parts.append((t * real[side], nz + side, c))
+        return total + sketch(parts)
+
+    total = lax.fori_loop(0, half, finish, total)
+
+    def settle():
+        def body(i, carry):
+            for side in range(2):
+                z = (0, top)[side]
+                c = i + (1 - side) * half
+
+                @pl.when(z_in[side])
+                def _(side=side):
+                    f_send(1 - side, i).wait_recv()
+
+                rws = pl.ds(at(c), step)
+                r[z, rws, :] = r[z, rws, :] + th[side, pl.ds(at(i), step), :]
+                r_save(z, c).start()
+            return carry
+        lax.fori_loop(0, half, body, 0)
+
+    def reduce(mine, axis, me, count, part, slots, ssem, rsem, between):
         part[...] = mine
         slots[me] = mine
 
@@ -260,11 +365,12 @@
             return carry
 
         lax.fori_loop(1, count, go, 0)
+        between()
         lax.fori_loop(1, count, land, 0)
         return lax.fori_loop(0, count, lambda i, acc: acc + slots[i], jnp.zeros_like(mine))
 
-    total = reduce(total[:rows], "gy", gy, n_gy, part_y, slots_y, s1s, s1r)
-    total = reduce(total, "gz", gz, n_gz, part_z, slots_z, s2s, s2r)
+    total = reduce(total[:rows], "gy", gy, n_gy, part_y, slots_y, s1s, s1r, lambda: None)
+    total = reduce(total, "gz", gz, n_gz, part_z, slots_z, s2s, s2r, settle)
     mean = jnp.sum(total * total) / (rows * blk)
     s_out[...] = total / jnp.sqrt(jnp.full((rows, blk), mean, F32) + 1e-06)
 
@@ -273,7 +379,13 @@
         @pl.when(z_out[side])
         def _(side=side):
             k_send(side).wait_send()
-            lax.fori_loop(0, nr, lambda c, x: (u_send(side, c).wait_send(), x)[1], 0)
+            for which in range(2):
+                o_send(side, which).wait_send()
+            lax.fori_loop(0, half, lambda i, x: (u_send(side, i).wait_send(), x)[1], 0)
+
+        @pl.when(z_in[side])
+        def _(side=side):
+            lax.fori_loop(0, half, lambda i, x: (f_send(side, i).wait_send(), x)[1], 0)
 
         @pl.when(y_out[side])
         def _(side=side):
@@ -297,32 +409,62 @@
     sent("gz", gz, n_gz, part_z, slots_z, s2s, s2r)
 
 
+def deliver(u_in, r_in, s_in, u_out, r_out, s_out, ub, rb, in_sem, out_sem):
+    pairs = []
+    nz, ny, nx = u_in.shape
+    n = in_sem.shape[0] // 2
+    for i in range(n):
+        rws = pl.ds(i * (ny // n), ny // n)
+        for j, (src, buf, dst) in enumerate(((u_in, ub, u_out), (r_in, rb, r_out))):
+            sem = 2 * i + j
+            pairs.append((
+                pltpu.make_async_copy(src.at[:, rws, :], buf.at[:, rws, :], in_sem.at[sem]),
+                pltpu.make_async_copy(buf.at[:, rws, :], dst.at[:, rws, :], out_sem.at[sem]),
+            ))
+    for load, _ in pairs:
+        load.start()
+    s_out[...] = s_in[...]
+    for load, store in pairs:
+        load.wait()
+        store.start()
+    for _, store in pairs:
+        store.wait()
+
+
 def shards(n_gz, n_gy, iterate, basis, coeffs, rhs, kappa, offsets, flips):
     nk, nz, ny, nx = basis.shape
     nq = offsets.shape[-1]
     blk = nx // nq
     rows = SK // blk
     nr = ny // 16
-    coef = lax.reduce_precision(coeffs, 8, 7)
+    half = nr // 2
+    hrows = half * 16
     dma = pltpu.SemaphoreType.DMA
     hbm = pl.BlockSpec(memory_space=pl.ANY)
     vmem = pl.BlockSpec(memory_space=pltpu.VMEM)
+    shapes = (
+        jax.ShapeDtypeStruct((nz, ny, nx), F32),
+        jax.ShapeDtypeStruct((nz, ny, nx), F32),
+        jax.ShapeDtypeStruct((rows, blk), F32),
+    )
     u, r, s = pl.pallas_call(
         functools.partial(kernel, n_gz, n_gy, blk, rows),
-        out_shape=(
-            jax.ShapeDtypeStruct((nz, ny, nx), F32),
-            jax.ShapeDtypeStruct((nz, ny, nx), F32),
-            jax.ShapeDtypeStruct((rows, blk), F32),
-        ),
+        out_shape=shapes,
         in_specs=[pl.BlockSpec(memory_space=pltpu.SMEM), hbm, hbm, hbm, hbm, vmem, vmem],
         out_specs=(hbm, hbm, vmem),
         scratch_shapes=[
             pltpu.VMEM((nk, nz, ny, nx), BF16),
+            pltpu.VMEM((nk, 16, blk), F32),
             pltpu.VMEM((nz, ny + 16, nx), F32),
             pltpu.VMEM((nz, ny + 16, nx), F32),
             pltpu.VMEM((nz, ny, nx), F32),
-            pltpu.VMEM((2, ny, nx), F32),
-            pltpu.VMEM((2, ny, nx), F32),
+            pltpu.VMEM((2, hrows, nx), F32),
+            pltpu.VMEM((2, hrows, nx), F32),
+            pltpu.VMEM((2, hrows, nx), F32),
+            pltpu.VMEM((2, hrows, nx), F32),
+            pltpu.VMEM((2, 2, nq, ny), jnp.int32),
+            pltpu.VMEM((nz + 2, ny, nq), jnp.int32),
+            pltpu.VMEM((nz + 2, ny, nq), F32),
             pltpu.VMEM((2, 2 * nz, nx), F32),
             pltpu.VMEM((2, 2 * nz, nx), F32),
             pltpu.VMEM((n_gy, rows, blk), F32),
@@ -331,10 +473,14 @@
             pltpu.VMEM((rows, blk), F32),
             dma((nz, nr)),
             dma((3,)),
-            dma((2, nr)),
-            dma((2, nr)),
+            dma((2, half)),
+            dma((2, half)),
             dma((2,)),
             dma((2,)),
+            dma((2, half)),
+            dma((2, half)),
+            dma((2, 2)),
+            dma((2, 2)),
             dma((2,)),
             dma((2,)),
             dma((n_gy,)),
@@ -346,9 +492,21 @@
         ],
         compiler_params=pltpu.CompilerParams(collective_id=0, has_side_effects=True),
     )(
-        coef, iterate, basis, rhs, kappa,
-        offsets.reshape(nz * ny, nq), flips.reshape(nz * ny, nq),
+        coeffs, iterate, basis, rhs, kappa,
+        offsets.transpose(0, 2, 1), flips.transpose(0, 2, 1),
     )
+    u, r, s = pl.pallas_call(
+        deliver,
+        out_shape=shapes,
+        in_specs=[hbm, hbm, vmem],
+        out_specs=(hbm, hbm, vmem),
+        scratch_shapes=[
+            pltpu.VMEM((nz, ny, nx), F32),
+            pltpu.VMEM((nz, ny, nx), F32),
+            dma((4,)),
+            dma((4,)),
+        ],
+    )(u, r, s)
     return u, r, s.reshape(SK)
 
 

time: 49.7 us -> 34.6 us (0.70)
  local copies, waits for them, and re-layouts: 7.91 us -> 0 us
  Pallas kernels: 39.6 us -> 33.7 us
  other arithmetic: 1.17 us -> 0 us
    pallas_call x1, Pallas kernels: 39.6 us -> 30.4 us  [shards(): pl.pallas_call(functools.partial(kernel, n_gz, n_gy, blk, rows), out_shap...]
    unnamed x5 -> x0, local copies, waits for them, and re-layouts: 7.91 us -> none
    pallas_call x0 -> x1, Pallas kernels: none -> 3.27 us  [shards(): pl.pallas_call(deliver, out_shape=shapes, in_specs=[hbm, hbm, vmem], out_...]
    reduce_precision x1 -> x0, other arithmetic: 1.17 us -> none  [shards(): coef = lax.reduce_precision(coeffs, 8, 7)]
where the time goes in v2:
time: 34.6 us; the launch traced here: 34.3 us
  Pallas kernels  33.7 us (97%)
  between operations  0.64 us (2%)
    pallas_call x1, Pallas kernels, shards(): pl.pallas_call(functools.partial(kernel, n_gz, n_gy, blk, rows), out_shap...  30.4 us
    pallas_call x1, Pallas kernels, shards(): pl.pallas_call(deliver, out_shape=shapes, in_specs=[hbm, hbm, vmem], out_...  3.27 us

profile of v2, /device:TPU:0, one launch (start us, length us, event | category | flops | bytes accessed | tf_op | source)
XLA Modules:
  0.0 34.3 jit_solution(4382855877031298840)
XLA Ops:
  0.6 30.4 %shard_map.94 = (f32[2,64,1024]{2,1,0:T(8,128)}, f32[2,64,1024]{2,1,0:T(8,128)}, f32[16,128]{1,0:T(8,128)}) custom-call(f32[32]{0:T(128)} %coef.1, f32[2,64,1024]{2,1,0:T(8,128)} %iterate.1, bf16[32,2,64,1024]{3,2,1,0:T(8,128)(2,1)} %basis.1, f32[2,64,1024]{2,1,0:T(8,128)} %rhs.1, f32[2,64,1024]{2,1,0:T(8,128)} %kappa.1, s32[2,8,64]{2,1,0:T(8,128)} %bitcast.3, ...), custom_call_target="tpu_custom_call" | custom-call | tf_op jit(solution)/shard_map/pallas_call | solution.py:450
  31.1 3.3 %shard_map.95 = (f32[2,64,1024]{2,1,0:T(8,128)}, f32[2,64,1024]{2,1,0:T(8,128)}, f32[16,128]{1,0:T(8,128)}) custom-call(f32[2,64,1024]{2,1,0:T(8,128)} %get-tuple-element.9.u_in, f32[2,64,1024]{2,1,0:T(8,128)} %get-tuple-element.10.r_in, f32[16,128]{1,0:T(8,128)} %get-tuple-element.11.s_in), custom_call_target="tpu_custom_call" | custom-call | tf_op jit(solution)/shard_map/pallas_call | solution.py:498

commit v3 on v2

--- a/solution.py
+++ b/solution.py
@@ -17,19 +17,20 @@
     n_gz, n_gy, blk, rows,
     coef, iterate, basis, rhs, kappa, offsets, flips,
     u_out, r_out, s_out,
-    bas, cf, u, k, r, uh, kh, tf, th, oh, offc, sgnc, ysend, yrecv,
+    bas, cf, u, k, r, uh, kh, tf, th, oh, lowb, hots, grid, ysend, yrecv,
     slots_y, slots_z, part_y, part_z,
     bas_sem, load_sem, us, ur, ks, kr, fs, fr, os_, or_, ys, yr, s1s, s1r, s2s, s2r,
     out_sem, uout_sem,
 ):
     nk, nz, ny, nx = basis.shape
     nq = nx // blk
-    shift = blk.bit_length() - 1
+    fine = 16
+    cells = rows * blk // fine
     step = 16
     nr = ny // step
     half = nr // 2
     hrows = half * step
-    assert nz >= 2 and ny == 2 * hrows and blk == 1 << shift
+    assert nz >= 2 and ny == 2 * hrows and cells <= blk and blk % fine == 0
     gz = lax.axis_index("gz")
     gy = lax.axis_index("gy")
     has_dn = gz > 0
@@ -75,6 +76,29 @@
 
     hail("gz", gz, n_gz)
     hail("gy", gy, n_gy)
+    col = lax.broadcasted_iota(jnp.int32, (step, blk), 1)
+
+    def prepare(p, off, flip, chunks):
+        off = off.T
+        sgn = (2 * flip - 1).astype(F32).T
+        for c in chunks:
+            rws = slice(c * step, (c + 1) * step)
+            cols = []
+            for q in range(nq):
+                o = jnp.broadcast_to(off[rws, q : q + 1], (step, blk))
+                s = jnp.broadcast_to(sgn[rws, q : q + 1], (step, blk))
+                lowb[p, rws, q * blk : (q + 1) * blk] = o & (fine - 1)
+                hi = o // fine
+                nxt = hi + blk // fine
+                nxt = jnp.where(nxt >= cells, nxt - cells, nxt)
+                cols.append(jnp.where(col == hi, s, 0.0).astype(BF16))
+                cols.append(jnp.where(col == nxt, s, 0.0).astype(BF16))
+            hots[p, c] = jnp.concatenate(cols, 0).T
+
+    for z in range(nz):
+        prepare(z, offsets[z], flips[z], range(nr))
+    for j in range(nk):
+        cf[j] = jnp.full((step, blk), coef[j], F32).astype(BF16).astype(F32)
     pl.semaphore_wait(barrier, n_gz - 1 + n_gy - 1)
 
     up = {"gz": lax.rem(gz + 1, n_gz)}
@@ -135,8 +159,6 @@
             for which in range(2):
                 o_send(side, which).start()
 
-    for j in range(nk):
-        cf[j] = jnp.full((step, blk), coef[j], F32).astype(BF16).astype(F32)
     u_load.wait()
 
     def combine(z, c):
@@ -236,56 +258,31 @@
             beyond = slice(8 + row, 8 + row + hrows)
             r[z, far, :] = r[z, far, :] - 0.5 * (k[z, beyond, :] * u[z, beyond, :])
 
-    def columns(p, off, flip):
-        offc[p] = off.T
-        sgnc[p] = (2 * flip - 1).astype(F32).T
-
-    for z in range(nz):
-        columns(z, offsets[z], flips[z])
-    for side in range(2):
-        @pl.when(z_in[side])
-        def _(side=side):
-            for which in range(2):
-                o_send(side, which).wait_recv()
-            k_send(side).wait_recv()
-        columns(nz + side, oh[side, 0], oh[side, 1])
-
-    col = lax.broadcasted_iota(jnp.int32, (step, blk), 1)
-
     def r_save(z, c):
         rws = pl.ds(at(c), step)
         return pltpu.make_async_copy(r.at[z, rws, :], r_out.at[z, rws, :], out_sem.at[z, c])
 
     def sketch(parts):
-        vals = []
-        hots = []
+        total = jnp.zeros((blk, blk), F32)
         for x_all, p, c in parts:
-            off = offc[p, pl.ds(at(c), step), :]
-            sgn = sgnc[p, pl.ds(at(c), step), :]
+            vals = []
             for q in range(nq):
-                o = jnp.broadcast_to(off[:, q : q + 1], (step, blk))
-                s = jnp.broadcast_to(sgn[:, q : q + 1], (step, blk))
-                x = x_all[:, q * blk : (q + 1) * blk] * s
-                low = o & (blk - 1)
+                x = x_all[:, q * blk : (q + 1) * blk]
+                low = lowb[p, pl.ds(at(c), step), q * blk : (q + 1) * blk]
                 bit = 1
-                while bit < blk:
+                while bit < fine:
                     x = jnp.where((low & bit) != 0, pltpu.roll(x, bit, 1), x)
                     bit *= 2
-                hi = lax.shift_right_logical(o, shift)
-                nxt = jnp.where(hi == rows - 1, 0, hi + 1)
                 keep = col >= low
                 vals.append(jnp.where(keep, x, 0.0))
                 vals.append(jnp.where(keep, 0.0, x))
-                hots.append(jnp.where(col == hi, 1.0, 0.0).astype(BF16))
-                hots.append(jnp.where(col == nxt, 1.0, 0.0).astype(BF16))
-        val = jnp.concatenate(vals, 0)
-        hot = jnp.concatenate(hots, 0)
-        big = val.astype(BF16)
-        small = (val - big.astype(F32)).astype(BF16)
-        dims = (((0,), (0,)), ((), ()))
-        return lax.dot_general(hot, big, dims, preferred_element_type=F32) + lax.dot_general(
-            hot, small, dims, preferred_element_type=F32
-        )
+            val = jnp.concatenate(vals, 0)
+            big = val.astype(BF16)
+            small = (val - big.astype(F32)).astype(BF16)
+            hot = hots[p, c]
+            total = total + jnp.dot(hot, big, preferred_element_type=F32)
+            total = total + jnp.dot(hot, small, preferred_element_type=F32)
+        return total
 
     def early(i, total):
         parts = [(r[top, pl.ds(at(i), step), :], top, i)]
@@ -298,6 +295,13 @@
 
     total = lax.fori_loop(0, half, early, jnp.zeros((blk, blk), F32))
     real = [jnp.where(z_in[side], 1.0, 0.0) for side in range(2)]
+    for side in range(2):
+        @pl.when(z_in[side])
+        def _(side=side):
+            for which in range(2):
+                o_send(side, which).wait_recv()
+            k_send(side).wait_recv()
+        prepare(nz + side, oh[side, 0], oh[side, 1], range(side * half, side * half + half))
 
     def finish(i, total):
         parts = []
@@ -326,7 +330,15 @@
             parts.append((t * real[side], nz + side, c))
         return total + sketch(parts)
 
-    total = lax.fori_loop(0, half, finish, total)
+    grid[...] = lax.fori_loop(0, half, finish, total)
+    total = jnp.zeros((rows, blk), F32)
+    lane = lax.broadcasted_iota(jnp.int32, (rows, blk), 1)
+    for d in range(blk // fine):
+        x = grid[pl.ds(d, rows, stride=blk // fine), :]
+        x = pltpu.roll(x, d * fine, 1) if d else x
+        total = total + jnp.where(lane >= d * fine, x, 0.0)
+        if d:
+            total = total + pltpu.roll(jnp.where(lane >= d * fine, 0.0, x), 1, 0)
 
     def settle():
         def body(i, carry):
@@ -369,7 +381,7 @@
         lax.fori_loop(1, count, land, 0)
         return lax.fori_loop(0, count, lambda i, acc: acc + slots[i], jnp.zeros_like(mine))
 
-    total = reduce(total[:rows], "gy", gy, n_gy, part_y, slots_y, s1s, s1r, lambda: None)
+    total = reduce(total, "gy", gy, n_gy, part_y, slots_y, s1s, s1r, lambda: None)
     total = reduce(total, "gz", gz, n_gz, part_z, slots_z, s2s, s2r, settle)
     mean = jnp.sum(total * total) / (rows * blk)
     s_out[...] = total / jnp.sqrt(jnp.full((rows, blk), mean, F32) + 1e-06)
@@ -463,8 +475,9 @@
             pltpu.VMEM((2, hrows, nx), F32),
             pltpu.VMEM((2, hrows, nx), F32),
             pltpu.VMEM((2, 2, nq, ny), jnp.int32),
-            pltpu.VMEM((nz + 2, ny, nq), jnp.int32),
-            pltpu.VMEM((nz + 2, ny, nq), F32),
+            pltpu.VMEM((nz + 2, ny, nx), jnp.int32),
+            pltpu.VMEM((nz + 2, nr, blk, 2 * nq * 16), BF16),
+            pltpu.VMEM((blk, blk), F32),
             pltpu.VMEM((2, 2 * nz, nx), F32),
             pltpu.VMEM((2, 2 * nz, nx), F32),
             pltpu.VMEM((n_gy, rows, blk), F32),

time: 34.6 us -> 35.5 us (1.026)
  Pallas kernels: 33.7 us -> 34.6 us
    pallas_call x1, Pallas kernels: 30.4 us -> 31.3 us  [shards(): pl.pallas_call(functools.partial(kernel, n_gz, n_gy, blk, rows), out_shap...]
where the time goes in v3:
time: 35.5 us; the launch traced here: 35.3 us
  Pallas kernels  34.6 us (97%)
  between operations  0.64 us (2%)
    pallas_call x1, Pallas kernels, shards(): pl.pallas_call(functools.partial(kernel, n_gz, n_gy, blk, rows), out_shap...  31.3 us
    pallas_call x1, Pallas kernels, shards(): pl.pallas_call(deliver, out_shape=shapes, in_specs=[hbm, hbm, vmem], out_...  3.27 us

profile of v3, /device:TPU:0, one launch (start us, length us, event | category | flops | bytes accessed | tf_op | source)
XLA Modules:
  0.0 35.3 jit_solution(6329415561616985916)
XLA Ops:
  0.6 31.3 %shard_map.94 = (f32[2,64,1024]{2,1,0:T(8,128)}, f32[2,64,1024]{2,1,0:T(8,128)}, f32[16,128]{1,0:T(8,128)}) custom-call(f32[32]{0:T(128)} %coef.1, f32[2,64,1024]{2,1,0:T(8,128)} %iterate.1, bf16[32,2,64,1024]{3,2,1,0:T(8,128)(2,1)} %basis.1, f32[2,64,1024]{2,1,0:T(8,128)} %rhs.1, f32[2,64,1024]{2,1,0:T(8,128)} %kappa.1, s32[2,8,64]{2,1,0:T(8,128)} %bitcast.3, ...), custom_call_target="tpu_custom_call" | custom-call | tf_op jit(solution)/shard_map/pallas_call | solution.py:462
  32.0 3.3 %shard_map.95 = (f32[2,64,1024]{2,1,0:T(8,128)}, f32[2,64,1024]{2,1,0:T(8,128)}, f32[16,128]{1,0:T(8,128)}) custom-call(f32[2,64,1024]{2,1,0:T(8,128)} %get-tuple-element.9.u_in, f32[2,64,1024]{2,1,0:T(8,128)} %get-tuple-element.10.r_in, f32[16,128]{1,0:T(8,128)} %get-tuple-element.11.s_in), custom_call_target="tpu_custom_call" | custom-call | tf_op jit(solution)/shard_map/pallas_call | solution.py:511

commit v4 on v3

--- a/solution.py
+++ b/solution.py
@@ -20,7 +20,7 @@
     bas, cf, u, k, r, uh, kh, tf, th, oh, lowb, hots, grid, ysend, yrecv,
     slots_y, slots_z, part_y, part_z,
     bas_sem, load_sem, us, ur, ks, kr, fs, fr, os_, or_, ys, yr, s1s, s1r, s2s, s2r,
-    out_sem, uout_sem,
+    out_sem, uout_sem, near,
 ):
     nk, nz, ny, nx = basis.shape
     nq = nx // blk
@@ -74,7 +74,14 @@
             return carry
         lax.fori_loop(1, count, body, 0)
 
-    hail("gz", gz, n_gz)
+    def tell(side, sem):
+        @pl.when((has_up, has_dn)[side])
+        def _():
+            dev = lax.rem(gz + (1, n_gz - 1)[side], n_gz)
+            pl.semaphore_signal(sem, inc=1, device_id={"gz": dev}, device_id_type=MESH)
+
+    for side in range(2):
+        tell(side, barrier)
     hail("gy", gy, n_gy)
     col = lax.broadcasted_iota(jnp.int32, (step, blk), 1)
 
@@ -95,11 +102,32 @@
                 cols.append(jnp.where(col == nxt, s, 0.0).astype(BF16))
             hots[p, c] = jnp.concatenate(cols, 0).T
 
-    for z in range(nz):
-        prepare(z, offsets[z], flips[z], range(nr))
     for j in range(nk):
         cf[j] = jnp.full((step, blk), coef[j], F32).astype(BF16).astype(F32)
-    pl.semaphore_wait(barrier, n_gz - 1 + n_gy - 1)
+    pl.semaphore_wait(barrier, n_gy - 1 + has_up.astype(jnp.int32) + has_dn.astype(jnp.int32))
+
+    rounds = max(n_gz - 2, 0)
+
+    def speak(t):
+        for side in range(2):
+            tell(side, near.at[side, t])
+
+    def hear(t):
+        for side in range(2):
+            @pl.when((has_dn, has_up)[side])
+            def _(side=side):
+                pl.semaphore_wait(near.at[side, t], 1)
+
+    state = {"said": 0, "heard": 0}
+
+    def gossip():
+        if state["heard"] < state["said"]:
+            hear(state["heard"])
+            state["heard"] += 1
+        if state["said"] < rounds:
+            speak(state["said"])
+            state["said"] += 1
+
 
     up = {"gz": lax.rem(gz + 1, n_gz)}
     dn = {"gz": lax.rem(gz + n_gz - 1, n_gz)}
@@ -158,6 +186,8 @@
             k_send(side).start()
             for which in range(2):
                 o_send(side, which).start()
+
+    gossip()
 
     u_load.wait()
 
@@ -187,7 +217,9 @@
         return carry
 
     lax.fori_loop(0, half, first, 0)
+    gossip()
     lax.fori_loop(0, half, second, 0)
+    gossip()
     u_save = pltpu.make_async_copy(u.at[:, pl.ds(8, ny), :], u_out, uout_sem.at[0])
     u_save.start()
     k_load.wait()
@@ -226,6 +258,9 @@
                 u[z, row : row + 1, :] = jnp.zeros((1, nx), F32)
                 k[z, row : row + 1, :] = jnp.zeros((1, nx), F32)
 
+    for z in range(nz):
+        prepare(z, offsets[z], flips[z], range(nr))
+    gossip()
     lane = lax.broadcasted_iota(jnp.int32, (step, nx), 1)
     for c in range(nr):
         y0 = 8 + c * step
@@ -249,6 +284,7 @@
             sl = slice(c * step, (c + 1) * step)
             r[z, sl, :] = r[z, sl, :] - 0.05 * uc - 0.5 * tot
 
+    gossip()
     for side in range(2):
         @pl.when(jnp.logical_not(z_in[side]))
         def _(side=side):
@@ -294,6 +330,7 @@
         return total + sketch(parts)
 
     total = lax.fori_loop(0, half, early, jnp.zeros((blk, blk), F32))
+    gossip()
     real = [jnp.where(z_in[side], 1.0, 0.0) for side in range(2)]
     for side in range(2):
         @pl.when(z_in[side])
@@ -330,7 +367,15 @@
             parts.append((t * real[side], nz + side, c))
         return total + sketch(parts)
 
+    gossip()
+
+    def more(i, carry):
+        speak(i)
+        hear(i)
+        return carry
+
     grid[...] = lax.fori_loop(0, half, finish, total)
+    lax.fori_loop(state["said"], rounds, more, 0)
     total = jnp.zeros((rows, blk), F32)
     lane = lax.broadcasted_iota(jnp.int32, (rows, blk), 1)
     for d in range(blk // fine):
@@ -502,6 +547,7 @@
             dma((n_gz,)),
             dma((nz, nr)),
             dma((1,)),
+            pltpu.SemaphoreType.REGULAR((2, max(n_gz - 2, 1))),
         ],
         compiler_params=pltpu.CompilerParams(collective_id=0, has_side_effects=True),
     )(

time: 35.5 us -> 35.3 us (level)
  no operation moved by 1% of the time
where the time goes in v4:
time: 35.3 us; the launch traced here: 35 us
  Pallas kernels  34.4 us (97%)
  between operations  0.64 us (2%)
    pallas_call x1, Pallas kernels, shards(): pl.pallas_call(functools.partial(kernel, n_gz, n_gy, blk, rows), out_shap...  31.1 us
    pallas_call x1, Pallas kernels, shards(): pl.pallas_call(deliver, out_shape=shapes, in_specs=[hbm, hbm, vmem], out_...  3.27 us

profile of v4, /device:TPU:0, one launch (start us, length us, event | category | flops | bytes accessed | tf_op | source)
XLA Modules:
  0.0 35.0 jit_solution(5195109006047499213)
XLA Ops:
  0.6 31.1 %shard_map.94 = (f32[2,64,1024]{2,1,0:T(8,128)}, f32[2,64,1024]{2,1,0:T(8,128)}, f32[16,128]{1,0:T(8,128)}) custom-call(f32[32]{0:T(128)} %coef.1, f32[2,64,1024]{2,1,0:T(8,128)} %iterate.1, bf16[32,2,64,1024]{3,2,1,0:T(8,128)(2,1)} %basis.1, f32[2,64,1024]{2,1,0:T(8,128)} %rhs.1, f32[2,64,1024]{2,1,0:T(8,128)} %kappa.1, s32[2,8,64]{2,1,0:T(8,128)} %bitcast.3, ...), custom_call_target="tpu_custom_call" | custom-call | tf_op jit(solution)/shard_map/pallas_call | solution.py:507
  31.8 3.3 %shard_map.95 = (f32[2,64,1024]{2,1,0:T(8,128)}, f32[2,64,1024]{2,1,0:T(8,128)}, f32[16,128]{1,0:T(8,128)}) custom-call(f32[2,64,1024]{2,1,0:T(8,128)} %get-tuple-element.9.u_in, f32[2,64,1024]{2,1,0:T(8,128)} %get-tuple-element.10.r_in, f32[16,128]{1,0:T(8,128)} %get-tuple-element.11.s_in), custom_call_target="tpu_custom_call" | custom-call | tf_op jit(solution)/shard_map/pallas_call | solution.py:557

commit v5 on v4

--- a/solution.py
+++ b/solution.py
@@ -356,10 +356,6 @@
             t = 0.5 * ((kc + kh[side, rws, :]) * (uc - uh[side, rws, :]))
             tf[side, rws, :] = t
 
-            @pl.when(z_in[side])
-            def _(side=side):
-                f_send(side, i).start()
-
             res = r[z, pl.ds(at(c), step), :] - t
             r[z, pl.ds(at(c), step), :] = res
             r_save(z, c).start()
@@ -386,6 +382,15 @@
             total = total + pltpu.roll(jnp.where(lane >= d * fine, 0.0, x), 1, 0)
 
     def settle():
+        def give(i, carry):
+            for side in range(2):
+                @pl.when(z_in[side])
+                def _(side=side):
+                    f_send(side, i).start()
+            return carry
+
+        lax.fori_loop(0, half, give, 0)
+
         def body(i, carry):
             for side in range(2):
                 z = (0, top)[side]

time: 35.3 us -> 34 us (0.963)
  the two profiles are of different devices: /device:TPU:0 before, /device:TPU:8 now
where the time goes in v5:
time: 34 us; the launch traced here: 33.6 us
  Pallas kernels  33 us (97%)
  between operations  0.64 us (2%)
    pallas_call x1, Pallas kernels, shards(): pl.pallas_call(functools.partial(kernel, n_gz, n_gy, blk, rows), out_shap...  29.7 us
    pallas_call x1, Pallas kernels, shards(): pl.pallas_call(deliver, out_shape=shapes, in_specs=[hbm, hbm, vmem], out_...  3.27 us

profile of v5, /device:TPU:8, one launch (start us, length us, event | category | flops | bytes accessed | tf_op | source)
XLA Modules:
  0.0 33.6 jit_solution(9431792929642209435)
XLA Ops:
  0.6 29.7 %shard_map.94 = (f32[2,64,1024]{2,1,0:T(8,128)}, f32[2,64,1024]{2,1,0:T(8,128)}, f32[16,128]{1,0:T(8,128)}) custom-call(f32[32]{0:T(128)} %coef.1, f32[2,64,1024]{2,1,0:T(8,128)} %iterate.1, bf16[32,2,64,1024]{3,2,1,0:T(8,128)(2,1)} %basis.1, f32[2,64,1024]{2,1,0:T(8,128)} %rhs.1, f32[2,64,1024]{2,1,0:T(8,128)} %kappa.1, s32[2,8,64]{2,1,0:T(8,128)} %bitcast.3, ...), custom_call_target="tpu_custom_call" | custom-call | tf_op jit(solution)/shard_map/pallas_call | solution.py:512
  30.4 3.3 %shard_map.95 = (f32[2,64,1024]{2,1,0:T(8,128)}, f32[2,64,1024]{2,1,0:T(8,128)}, f32[16,128]{1,0:T(8,128)}) custom-call(f32[2,64,1024]{2,1,0:T(8,128)} %get-tuple-element.9.u_in, f32[2,64,1024]{2,1,0:T(8,128)} %get-tuple-element.10.r_in, f32[16,128]{1,0:T(8,128)} %get-tuple-element.11.s_in), custom_call_target="tpu_custom_call" | custom-call | tf_op jit(solution)/shard_map/pallas_call | solution.py:562
